TPU v7x, 1024 devices: a whole 4x4x32 slice. The times are simulated.
1024 devices in a mesh: fsdp: 32 (over z_hi, x, core), ctx: 32 (over y, z_lo).
Axes of the slice: x: 4, y: 4, z: 32 (z_hi: 4, z_lo: 8; z = z_hi * 8 + z_lo), core: 2. Of those that a mesh axis runs over, the one named last changes fastest.
Arguments:
- queries: bfloat16 [32, 4096, 2048], P('fsdp', 'ctx'), may hold values from -200 to 200
- keyvals: bfloat16 [32, 4096, 2, 512], P('fsdp', 'ctx'), may hold values from -6 to 6
- span_ids: int32 [32, 64], P('fsdp'), may hold values from 0 to 63, as said below
Outputs:
- attended: bfloat16 [32, 4096, 2048], P('fsdp', 'ctx')
Inputs may be any that keep to these rules, and one draw needn't show every extreme that they name: `span_ids`: in each sequence, ctx device d holds storage spans 2d and 2d+1; storage span 2d has position span p with p < 32 and storage span 2d+1 has position span 64 - 1-p; each p belongs to exactly one device.
All inputs are finite; a program needn't handle non-finite values.
Results may differ from a plain program's by a relative error of at most 0.0041.
Values may be sent and summed in bfloat16 or wider, within the bound.
A program may use at most 64 MiB of HBM per device.

v0:
```python
import math

import jax
import jax.numpy as jnp
from jax import lax
from jax.sharding import PartitionSpec as P

KV_HEADS = 4
GROUP = 4
HEAD_DIM = 128


def attend_slot(state, slot_rows, slot_pos, buffer, base):
    buffer_rows = buffer.shape[0]
    key_heads = slot_rows.shape[0]
    head_width = slot_rows.shape[2]
    block_width = math.gcd(buffer_rows, 512)
    total_blocks = buffer_rows // block_width
    scale = 1.0 / math.sqrt(head_width)
    needed = (jnp.max(slot_pos) + 1 - base + block_width - 1) // block_width
    block_total = jnp.clip(needed, 0, total_blocks)
    inside = jnp.arange(block_width, dtype=jnp.int32)

    def visit(block, carry):
        running_max, running_sum, weighted = carry
        rows = lax.dynamic_slice_in_dim(buffer, block * block_width, block_width, 0)
        key_block = rows[:, 0].reshape(block_width, key_heads, head_width)
        value_block = rows[:, 1].reshape(block_width, key_heads, head_width)
        key_pos = base + block * block_width + inside
        scores = (
            jnp.einsum("hrd,nhd->hrn", slot_rows, key_block, preferred_element_type=jnp.float32)
            * scale
        )
        allowed = key_pos[None, None, :] <= slot_pos[None, :, None]
        scores = jnp.where(allowed, scores, -1e30)
        new_max = jnp.maximum(running_max, jnp.max(scores, axis=-1))
        shrink = jnp.exp(running_max - new_max)
        weights = jnp.where(allowed, jnp.exp(scores - new_max[..., None]), 0.0)
        running_sum = running_sum * shrink + jnp.sum(weights, axis=-1)
        update = jnp.einsum(
            "hrn,nhd->hrd",
            weights.astype(jnp.bfloat16),
            value_block,
            preferred_element_type=jnp.float32,
        )
        weighted = weighted * shrink[..., None] + update
        return (new_max, running_sum, weighted)

    return lax.fori_loop(0, block_total, visit, state)


def per_device(queries, keyvals, span_ids):
    tok_rows = queries.shape[1]
    span_rows = tok_rows // 2
    ctx_count = lax.axis_size("ctx")
    seq_rows = tok_rows * ctx_count
    key_heads = KV_HEADS
    group_size = GROUP
    head_width = HEAD_DIM
    feature_width = key_heads * head_width
    span_table = span_ids[0]
    device_index = lax.axis_index("ctx")
    own_spans = lax.dynamic_slice_in_dim(span_table, 2 * device_index, 2)
    offsets = jnp.arange(span_rows, dtype=jnp.int32)
    query_pos = (
        own_spans[:, None, None] * span_rows
        + jnp.zeros((1, group_size, 1), jnp.int32)
        + offsets[None, None, :]
    ).reshape(2, group_size * span_rows)
    query_rows = queries[0].reshape(2, span_rows, key_heads, group_size, head_width)
    query_rows = jnp.transpose(query_rows, (2, 0, 3, 1, 4)).reshape(
        key_heads, 2, group_size * span_rows, head_width
    )
    slot_count = group_size * span_rows

    def fresh_state():
        return (
            jnp.full((key_heads, slot_count), -1e30, jnp.float32),
            jnp.zeros((key_heads, slot_count), jnp.float32),
            jnp.zeros((key_heads, slot_count, head_width), jnp.float32),
        )

    empty = jnp.zeros((seq_rows, 2, feature_width), jnp.bfloat16)
    piece_rows = lax.all_gather(keyvals, "ctx", axis=1, tiled=True)[0]
    span_total = piece_rows.shape[0] // span_rows

    def place_one(index, current):
        position_span = lax.dynamic_index_in_dim(span_table, index, 0, False)
        rows = lax.dynamic_slice_in_dim(piece_rows, index * span_rows, span_rows, 0)
        return lax.dynamic_update_slice_in_dim(current, rows, position_span * span_rows, 0)

    buffer = lax.fori_loop(0, span_total, place_one, empty)
    first_state = attend_slot(fresh_state(), query_rows[:, 0], query_pos[0], buffer, 0)
    second_state = attend_slot(fresh_state(), query_rows[:, 1], query_pos[1], buffer, 0)
    finished = []
    for state in (first_state, second_state):
        running_max, running_sum, weighted = state
        finished.append(weighted / running_sum[..., None])
    result = jnp.stack(finished, axis=1)
    result = result.reshape(key_heads, 2, group_size, span_rows, head_width)
    attended = (
        jnp.transpose(result, (1, 3, 0, 2, 4))
        .reshape(1, tok_rows, key_heads * group_size * head_width)
        .astype(jnp.bfloat16)
    )
    return attended


def solution(mesh):
    in_specs = (P("fsdp", "ctx", None), P("fsdp", "ctx", None, None), P("fsdp", None))
    out_specs = P("fsdp", "ctx", None)
    return jax.shard_map(
        per_device, mesh=mesh, in_specs=in_specs, out_specs=out_specs, check_vma=False
    )
```

profile of v0, /device:TPU:4, one launch (start us, length us, event | category | flops | bytes accessed | tf_op | source)
XLA Modules:
  0.0 537.1 jit_solution(18353677302877855894)
XLA Ops:
  11.7 271.4 %all-gather.2.cloned.1.call-done = bf16[1,4096,2,512]{3,2,0,1:T(2,128)(2,1)} async-done(((bf16[1,128,2,512]{3,2,0,1:T(2,128)(2,1)}), bf16[1,4096,2,512]{3,2,0,1:T(2,128)(2,1)}) %all-gather.2.cloned.1.call-update) | async-done | bytes 8388624 | tf_op jit(solution)/shard_map/all_gather | solution.py:84
  283.1 5.4 %broadcast_in_dim.45 = bf16[4096,2,512]{2,1,0:T(2,128)(2,1)} broadcast(bf16[]{:T(256)} %constant.119.clone.1), dimensions={} | broadcast | bytes 8388610 | tf_op jit(solution)/shard_map/broadcast_in_dim | solution.py:83
  288.5 184.4 %while.43 = (s32[]{:T(128)}, bf16[4096,2,512]{2,1,0:T(2,128)(2,1)}, bf16[4096,2,512]{2,1,0:T(2,128)(2,1)}, s32[64]{0:T(128)S(1)}, s32[]{:T(128)}, /*index=5*/s32[1]{0:T(128)}, s32[]{:T(128)}, s32[]{:T(128)}, s32[]{:T(128)}) while((s32[]{:T(128)}, bf16[4096,2,512]{2,1,0:T(2,128)(2,1)}, bf16[4096,2,512]{2,1,0:T(2,128)(2,1)}, s32[64]{0:T(128)S(1)}, ...), condition=%wide.region_2.3_spmd, body=%wide.region_1.2_spmd.sunk | while | flops 10 | bytes 262349 | solution.py:92
  292.7 1.7 dynamic-slice_dynamic-update-slice_fusion.2
  295.5 1.7 dynamic-slice_dynamic-update-slice_fusion.2
  304.2 1.7 dynamic-slice_dynamic-update-slice_fusion.2
  315.7 1.7 dynamic-slice_dynamic-update-slice_fusion.2
  318.6 1.7 dynamic-slice_dynamic-update-slice_fusion.2
  324.4 1.7 dynamic-slice_dynamic-update-slice_fusion.2
  327.2 1.7 dynamic-slice_dynamic-update-slice_fusion.2
  333.0 1.7 dynamic-slice_dynamic-update-slice_fusion.2
  341.7 1.7 dynamic-slice_dynamic-update-slice_fusion.2
  347.4 1.7 dynamic-slice_dynamic-update-slice_fusion.2
  359.0 1.7 dynamic-slice_dynamic-update-slice_fusion.2
  364.7 1.7 dynamic-slice_dynamic-update-slice_fusion.2
  376.2 1.7 dynamic-slice_dynamic-update-slice_fusion.2
  384.9 1.7 dynamic-slice_dynamic-update-slice_fusion.2
  387.7 1.7 dynamic-slice_dynamic-update-slice_fusion.2
  396.4 1.7 dynamic-slice_dynamic-update-slice_fusion.2
  407.9 1.7 dynamic-slice_dynamic-update-slice_fusion.2
  410.8 1.7 dynamic-slice_dynamic-update-slice_fusion.2
  413.7 1.7 dynamic-slice_dynamic-update-slice_fusion.2
  433.8 1.7 dynamic-slice_dynamic-update-slice_fusion.2
  445.3 1.7 dynamic-slice_dynamic-update-slice_fusion.2
  448.2 1.7 dynamic-slice_dynamic-update-slice_fusion.2
  454.0 1.7 dynamic-slice_dynamic-update-slice_fusion.2
  459.8 1.7 dynamic-slice_dynamic-update-slice_fusion.2
  465.5 1.7 dynamic-slice_dynamic-update-slice_fusion.2
  468.4 1.7 dynamic-slice_dynamic-update-slice_fusion.2
  472.9 21.3 %copy.28 = bf16[4096,2,512]{0,2,1:T(8,128)(2,1)} copy(bf16[4096,2,512]{2,1,0:T(2,128)(2,1)} %get-tuple-element.255) | data formatting | bytes 16777216
  494.3 11.2 %while.44 = (s32[]{:T(128)}, f32[4,256]{1,0:T(4,128)S(1)}, f32[4,256]{1,0:T(4,128)S(1)}, f32[4,256,128]{2,1,0:T(8,128)S(1)}, s32[]{:T(128)}, /*index=5*/s32[1,25...) while((s32[]{:T(128)}, f32[4,256]{1,0:T(4,128)S(1)}, ...), condition=%wide.region_6.7_spmd.clone, body=%wide.region_3.6_spmd.clone.sunk | while | flops 275646976 | bytes 11343043 | solution.py:49
  505.9 22.3 %while.45 = (s32[]{:T(128)}, f32[4,256]{1,0:T(4,128)S(1)}, f32[4,256]{1,0:T(4,128)S(1)}, f32[4,256,128]{2,1,0:T(8,128)S(1)}, s32[]{:T(128)}, /*index=5*/s32[1,25...) while((s32[]{:T(128)}, f32[4,256]{1,0:T(4,128)S(1)}, ...), condition=%wide.region_11.12_spmd.clone, body=%wide.region_8.11_spmd.clone.sunk | while | flops 275646976 | bytes 11343043 | solution.py:49
  (207 shorter events, 139.6 us)
Async XLA Ops:
  6.5 276.6 %all-gather.2.cloned.1.call-start = ((), (), s32[]{:S(2)}) async-start(), calls=%async_computation | async-start | bytes 8650752 | tf_op jit(solution)/shard_map/all_gather | solution.py:84
  283.1 5.4 %copy-start = (s32[1,64]{1,0:T(1,128)S(1)}, s32[1,64]{1,0:T(1,128)}, u32[]{:S(2)}) copy-start(s32[1,64]{1,0:T(1,128)} %param.11) | copy-start | bytes 772
Sparse Core Ops, SparseCore 0:
  10.0 273.0 all-gather.1
where the time goes:
time: 540 us; the launch traced here: 537 us
  waiting for transfers between devices  272 us (50%)
  local copies, waits for them, and re-layouts  185 us (34%)
  loops' own time  41.6 us (8%)
  matrix products  15 us (3%)
  between operations  14.8 us (3%)
  other arithmetic  8.49 us (2%)
    all_gather x1, waiting for transfers between devices, per_device(): piece_rows = lax.all_gather(keyvals, 'ctx', axis=1, tiled=True)[0]  271 us
    dynamic_update_slice x64, local copies, waits for them, and re-layouts, place_one(): lax.dynamic_update_slice_in_dim(current, rows, position_span * span_rows, 0)  106 us
    another operation x1, loops' own time, per_device(): buffer = lax.fori_loop(0, span_total, place_one, empty)  40.9 us
    dynamic_slice x64, local copies, waits for them, and re-layouts, place_one(): position_span = lax.dynamic_index_in_dim(span_table, index, 0, False)  37.9 us
    unnamed x3, local copies, waits for them, and re-layouts  21.3 us
    slice x9, local copies, waits for them, and re-layouts, visit(): value_block = rows[:, 1].reshape(block_width, key_heads, head_width)  11.5 us
  transfers between devices with their start and end apart: 1, of which 1 were waited for; matrix products, arithmetic and copies ran while one was open for 1% of the time, Pallas kernels for 0%

commit v1 on v0

v1 whole, which is shorter than its diff:
```python
import functools
import math

import jax
import jax.numpy as jnp
from jax import lax
from jax.experimental import pallas as pl
from jax.experimental.pallas import tpu as pltpu
from jax.sharding import PartitionSpec as P

HEADS = 4
GROUP = 4
DIM = 128
SPAN = 64
ROWS = 2 * SPAN
NEG = -1e30
MESH = pl.DeviceIdType.MESH
FACTOR = math.log2(math.e) / math.sqrt(DIM)


def gray(j):
    return j + (j // 2) * (5 - 2 * j)


def kernel(
    nz, ids_ref, q_ref, kv_ref, out_ref,
    kv_buf, q_buf, o_buf, gap, acc, total, top,
    recv, right_sem, left_sem, kv_sem, q_sem, q_recv, o_sem, o_recv, own_sem,
):
    me = lax.axis_index("ctx")
    y, z = me // nz, me % nz
    has_left, has_right = z > 0, z < nz - 1
    width = GROUP * DIM
    keys = HEADS * SPAN

    def device(yy, zz):
        return {"ctx": yy * nz + zz}

    def remote(src, dst, send, receive, where):
        return pltpu.make_async_remote_copy(
            src_ref=src, dst_ref=dst, send_sem=send, recv_sem=receive,
            device_id=where, device_id_type=MESH,
        )

    def piece(zz, yy):
        return kv_buf.at[zz, :, :, yy]

    def columns(yy):
        return pl.ds(pl.multiple_of(yy * width, width), width)

    def other(d):
        return (y + d) % HEADS

    barrier = pltpu.get_barrier_semaphore()
    for d in (1, 2, 3):
        pl.semaphore_signal(barrier, inc=1, device_id=device(other(d), z), device_id_type=MESH)

    @pl.when(has_left)
    def _():
        pl.semaphore_signal(barrier, inc=1, device_id=device(y, z - 1), device_id_type=MESH)

    @pl.when(has_right)
    def _():
        pl.semaphore_signal(barrier, inc=1, device_id=device(y, z + 1), device_id_type=MESH)

    pl.semaphore_wait(barrier, 3 + (z + nz - 1) // nz + (2 * nz - 2 - z) // nz)

    def to_right(src, zz, yy):
        return remote(src, piece(zz, yy), right_sem.at[zz, yy], recv.at[zz, yy], device(y, z + 1))

    def to_left(src, zz, yy):
        return remote(src, piece(zz, yy), left_sem.at[zz, yy], recv.at[zz, yy], device(y, z - 1))

    def arrived(zz, yy):
        remote(piece(zz, yy), piece(zz, yy), recv.at[zz, yy], recv.at[zz, yy], device(y, z)).wait_recv()

    @pl.when(has_right)
    def _():
        to_right(kv_ref.at[y], z, y).start()

    @pl.when(has_left)
    def _():
        to_left(kv_ref.at[y], z, y).start()

    kv_sends = [
        remote(kv_ref.at[other(d)], piece(z, y), kv_sem.at[d - 1], recv.at[z, y], device(other(d), z))
        for d in (1, 3, 2)
    ]
    for copy in kv_sends:
        copy.start()
    own_kv = pltpu.make_async_copy(kv_ref.at[y], piece(z, y), own_sem.at[0])
    own_kv.start()
    q_sends = [
        remote(
            q_ref.at[:, columns(other(d))], q_buf.at[y], q_sem.at[d - 1], q_recv.at[y], device(other(d), z)
        )
        for d in (1, 3, 2)
    ]
    for copy in q_sends:
        copy.start()
    own_q = pltpu.make_async_copy(q_ref.at[:, columns(y)], q_buf.at[y], own_sem.at[1])
    own_q.start()

    for d in (1, 3, 2):
        arrived(z, other(d))

        @pl.when(has_right)
        def _():
            to_right(piece(z, other(d)), z, other(d)).start()

        @pl.when(has_left)
        def _():
            to_left(piece(z, other(d)), z, other(d)).start()

    lane = lax.broadcasted_iota(jnp.int32, (SPAN, keys), 1)
    row = lax.broadcasted_iota(jnp.int32, (SPAN, keys), 0)
    base = lane % SPAN - row

    def fill(zz, carry):
        for half in range(2):
            span = jnp.zeros((SPAN, keys), jnp.int32)
            for yy in range(HEADS):
                span = jnp.where(lane // SPAN == yy, ids_ref[0, 2 * (yy * nz + zz) + half], span)
            gap[zz, half] = span * SPAN + base
        return carry

    lax.fori_loop(0, nz, fill, 0)
    top[...] = jnp.full(top.shape, NEG, jnp.float32)
    total[...] = jnp.zeros(total.shape, jnp.float32)
    acc[...] = jnp.zeros(acc.shape, jnp.float32)
    own_kv.wait()
    own_q.wait()

    def product(a, b):
        return lax.dot_general(a, b, (((1,), (1,)), ((), ())), preferred_element_type=jnp.float32)

    def update(yq, rows, scores, values):
        best = scores[0]
        for s in scores[1:]:
            best = jnp.maximum(best, s)
        old = top[yq, rows]
        new = jnp.maximum(old, jnp.max(best, axis=-1, keepdims=True))
        shrink = jnp.exp2((old - new) * FACTOR)
        wide = jnp.concatenate([new] * (keys // DIM), axis=-1)
        weighted = acc[yq, rows] * shrink
        summed = total[yq, rows] * shrink
        for s, v in zip(scores, values):
            p = jnp.exp2((s - wide) * FACTOR)
            for k in range(keys // DIM):
                summed = summed + p[:, k * DIM : (k + 1) * DIM]
            weighted = weighted + jnp.dot(p.astype(jnp.bfloat16), v, preferred_element_type=jnp.float32)
        acc[yq, rows] = weighted
        total[yq, rows] = summed
        top[yq, rows] = new

    def attend(yq, zz):
        low_k, high_k, low_v, high_v = (
            kv_buf[zz, a, b].reshape(keys, DIM) for a in range(2) for b in range(2)
        )
        low_q, high_q = (
            jnp.concatenate(
                [q_buf[yq, b * SPAN : (b + 1) * SPAN, g * DIM : (g + 1) * DIM] for g in range(GROUP)], axis=0
            )
            for b in range(2)
        )
        home = 2 * (yq * nz + z)

        def masked(s, half):
            distance = jnp.concatenate([gap[zz, half]] * GROUP, axis=0)
            return jnp.where(distance <= ids_ref[0, home + half] * SPAN, s, NEG)

        half_rows = GROUP * SPAN
        update(yq, pl.ds(0, half_rows), [masked(product(low_q, low_k), 0)], [low_v])
        update(
            yq, pl.ds(half_rows, half_rows),
            [product(high_q, low_k), masked(product(high_q, high_k), 1)], [low_v, high_v],
        )

    def both_sides(yq, step):
        @pl.when(z - step >= 0)
        def _():
            attend(yq, z - step)

        @pl.when(jnp.logical_and(z + step < nz, step > 0))
        def _():
            attend(yq, z + step)

    def advance(step, carry):
        def part(j, inner):
            yy = other(gray(j))

            @pl.when(z - step >= 0)
            def _():
                arrived(z - step, yy)

                @pl.when(has_right)
                def _():
                    to_right(piece(z - step, yy), z - step, yy).start()

            @pl.when(z + step < nz)
            def _():
                arrived(z + step, yy)

                @pl.when(has_left)
                def _():
                    to_left(piece(z + step, yy), z + step, yy).start()

            @pl.when(jnp.logical_and(step == 1, j > 0))
            def _():
                remote(q_buf.at[yy], q_buf.at[yy], q_recv.at[yy], q_recv.at[yy], device(y, z)).wait_recv()

            both_sides(yy, step - 1)
            return inner

        return lax.fori_loop(0, HEADS, part, carry)

    lax.fori_loop(1, nz, advance, 0)

    def finish(j, carry):
        yq = other(gray(HEADS - 1 - j))
        both_sides(yq, nz - 1)
        out = acc[yq] / jnp.sum(total[yq], axis=-1, keepdims=True)
        out = out.astype(jnp.bfloat16)
        for b in range(2):
            for g in range(GROUP):
                start = (b * GROUP + g) * SPAN
                o_buf[yq, b * SPAN : (b + 1) * SPAN, g * DIM : (g + 1) * DIM] = out[start : start + SPAN]

        @pl.when(j < HEADS - 1)
        def _():
            remote(
                o_buf.at[yq], out_ref.at[:, columns(y)], o_sem.at[yq], o_recv.at[y], device(yq, z)
            ).start()

        return carry

    lax.fori_loop(0, HEADS, finish, 0)
    own_o = pltpu.make_async_copy(o_buf.at[y], out_ref.at[:, columns(y)], own_sem.at[2])
    own_o.start()

    for copy in kv_sends + q_sends:
        copy.wait_send()

    def drain(yy, carry):
        @pl.when(has_right)
        def _():
            def one(zz, inner):
                to_right(piece(zz, yy), zz, yy).wait_send()
                return inner

            lax.fori_loop(0, z + 1, one, 0)

        @pl.when(has_left)
        def _():
            def one(zz, inner):
                to_left(piece(zz, yy), zz, yy).wait_send()
                return inner

            lax.fori_loop(z, nz, one, 0)

        return carry

    lax.fori_loop(0, HEADS, drain, 0)
    for d in (1, 2, 3):
        yy = other(d)
        copy = remote(o_buf.at[yy], out_ref.at[:, columns(yy)], o_sem.at[yy], o_recv.at[yy], device(yy, z))
        copy.wait_send()
        copy.wait_recv()
    own_o.wait()


def per_device(queries, keyvals, span_ids):
    nz = lax.axis_size("ctx") // HEADS
    q = queries[0]
    kv = keyvals[0].reshape(2, SPAN, 2, HEADS, DIM).transpose(3, 2, 0, 1, 4)
    rows = 2 * GROUP * SPAN
    dma = pltpu.SemaphoreType.DMA
    flops = 4 * HEADS * rows * DIM * nz * HEADS * ROWS
    out = pl.pallas_call(
        functools.partial(kernel, nz),
        out_shape=jax.ShapeDtypeStruct(q.shape, jnp.bfloat16),
        in_specs=[
            pl.BlockSpec(memory_space=pltpu.SMEM),
            pl.BlockSpec(memory_space=pl.ANY),
            pl.BlockSpec(memory_space=pl.ANY),
        ],
        out_specs=pl.BlockSpec(memory_space=pl.ANY),
        scratch_shapes=[
            pltpu.VMEM((nz, 2, 2, HEADS, SPAN, DIM), jnp.bfloat16),
            pltpu.VMEM((HEADS, ROWS, GROUP * DIM), jnp.bfloat16),
            pltpu.VMEM((HEADS, ROWS, GROUP * DIM), jnp.bfloat16),
            pltpu.VMEM((nz, 2, SPAN, HEADS * SPAN), jnp.int32),
            pltpu.VMEM((HEADS, rows, DIM), jnp.float32),
            pltpu.VMEM((HEADS, rows, DIM), jnp.float32),
            pltpu.VMEM((HEADS, rows, DIM), jnp.float32),
            dma((nz, HEADS)), dma((nz, HEADS)), dma((nz, HEADS)),
            dma((3,)), dma((3,)), dma((HEADS,)), dma((HEADS,)), dma((HEADS,)), dma((3,)),
        ],
        compiler_params=pltpu.CompilerParams(
            collective_id=0, has_side_effects=True, vmem_limit_bytes=48 * 1024 * 1024
        ),
        cost_estimate=pl.CostEstimate(flops=flops, bytes_accessed=4 * 1024 * 1024, transcendentals=0),
        name="attend",
    )(span_ids, q, kv)
    return out[None]


def solution(mesh):
    in_specs = (P("fsdp", "ctx", None), P("fsdp", "ctx", None, None), P("fsdp", None))
    return jax.shard_map(
        per_device, mesh=mesh, in_specs=in_specs, out_specs=P("fsdp", "ctx", None), check_vma=False
    )
```

time: 540 us -> 63.6 us (0.12)
  the two profiles are of different devices: /device:TPU:4 before, /device:TPU:8 now
where the time goes in v1:
time: 63.6 us; the launch traced here: 63.4 us
  Pallas kernels  60.7 us (95%)
  local copies, waits for them, and re-layouts  2.66 us (4%)
    pallas_call x1, Pallas kernels, per_device(): pl.pallas_call(functools.partial(kernel, nz), out_shape=jax.ShapeDtypeStr...  60.7 us
    unnamed x5, local copies, waits for them, and re-layouts  1.44 us

profile of v1, /device:TPU:8, one launch (start us, length us, event | category | flops | bytes accessed | tf_op | source)
XLA Modules:
  0.0 63.4 jit_solution(1935714237676312661)
XLA Ops:
  0.0 0.0 copy-start
  0.0 1.2 %reshape = bf16[2,64,2,4,128]{4,3,2,1,0:T(4,128)(2,1)S(1)} reshape(bf16[1,128,2,512]{3,2,1,0:T(2,128)(2,1)} %param.4) | data formatting | bytes 524288 | tf_op jit(solution)/shard_map/reshape;squeeze | solution.py:275
  1.2 0.0 copy-start.1
  1.2 0.0 copy-done
  1.3 0.6 %copy-done.1 = s32[1,64]{1,0:T(1,128)S(1)} copy-done((s32[1,64]{1,0:T(1,128)S(1)}, s32[1,64]{1,0:T(1,128)}, u32[]{:S(2)}) %copy-start.1) | copy-done | bytes 280
  1.9 60.7 %attend.1 = bf16[128,2048]{1,0:T(8,128)(2,1)S(1)} custom-call(s32[1,64]{1,0:T(1,128)S(1)} %copy-done.1, bf16[128,2048]{1,0:T(8,128)(2,1)S(1)} %bitcast.7, bf16[4,2,2,64,128]{4,3,2,1,0:T(8,128)(2,1)S(1)} %bitcast.6), custom_call_target="tpu_custom_call" | custom-call | flops 4294967296 | bytes 4194304 | tf_op jit(solution)/shard_map/attend/pallas_call | solution.py:279
  62.6 0.8 %copy.11 = bf16[1,128,2048]{2,1,0:T(8,128)(2,1)} copy(bf16[1,128,2048]{2,1,0:T(8,128)(2,1)S(1)} %bitcast.5) | data formatting | bytes 1048576
  (1 shorter events, 0.0 us)
Async XLA Ops:
  0.0 1.2 %copy-start = (bf16[1,128,2048]{2,1,0:T(8,128)(2,1)S(1)}, bf16[1,128,2048]{2,1,0:T(8,128)(2,1)}, u32[]{:S(2)}) copy-start(bf16[1,128,2048]{2,1,0:T(8,128)(2,1)} %param.3) | copy-start | bytes 1572868
  1.2 0.7 %copy-start.1 = (s32[1,64]{1,0:T(1,128)S(1)}, s32[1,64]{1,0:T(1,128)}, u32[]{:S(2)}) copy-start(s32[1,64]{1,0:T(1,128)} %ids_ref.1) | copy-start | bytes 772

commit v2 on v1

--- a/solution.py
+++ b/solution.py
@@ -176,14 +176,14 @@
             [product(high_q, low_k), masked(product(high_q, high_k), 1)], [low_v, high_v],
         )
 
-    def both_sides(yq, step):
-        @pl.when(z - step >= 0)
-        def _():
-            attend(yq, z - step)
-
-        @pl.when(jnp.logical_and(z + step < nz, step > 0))
-        def _():
-            attend(yq, z + step)
+    rightward = (3 * nz - 2 - 2 * z) // (2 * nz)
+    shorter = rightward * z + (1 - rightward) * (nz - 1 - z)
+
+    def column(t):
+        in_turn = (2 * shorter - t + 2 * nz) // (2 * nz)
+        near = (1 - 2 * (t % 2)) * ((t + 1) // 2)
+        far = (2 * rightward - 1) * (t - shorter)
+        return z + in_turn * near + (1 - in_turn) * far
 
     def advance(step, carry):
         def part(j, inner):
@@ -209,7 +209,7 @@
             def _():
                 remote(q_buf.at[yy], q_buf.at[yy], q_recv.at[yy], q_recv.at[yy], device(y, z)).wait_recv()
 
-            both_sides(yy, step - 1)
+            attend(yy, column(step - 1))
             return inner
 
         return lax.fori_loop(0, HEADS, part, carry)
@@ -218,7 +218,7 @@
 
     def finish(j, carry):
         yq = other(gray(HEADS - 1 - j))
-        both_sides(yq, nz - 1)
+        attend(yq, column(nz - 1))
         out = acc[yq] / jnp.sum(total[yq], axis=-1, keepdims=True)
         out = out.astype(jnp.bfloat16)
         for b in range(2):

time: 63.6 us -> 62.5 us (0.983)
  Pallas kernels: 60.7 us -> 59.6 us
    pallas_call x1, Pallas kernels: 60.7 us -> 59.6 us  [per_device(): pl.pallas_call(functools.partial(kernel, nz), out_shape=jax.ShapeDtypeStr...]
where the time goes in v2:
time: 62.5 us; the launch traced here: 62.3 us
  Pallas kernels  59.6 us (95%)
  local copies, waits for them, and re-layouts  2.66 us (4%)
    pallas_call x1, Pallas kernels, per_device(): pl.pallas_call(functools.partial(kernel, nz), out_shape=jax.ShapeDtypeStr...  59.6 us
    unnamed x5, local copies, waits for them, and re-layouts  1.44 us

profile of v2, /device:TPU:8, one launch (start us, length us, event | category | flops | bytes accessed | tf_op | source)
XLA Modules:
  0.0 62.3 jit_solution(7709335691025345720)
XLA Ops:
  0.0 0.0 copy-start
  0.0 1.2 %reshape = bf16[2,64,2,4,128]{4,3,2,1,0:T(4,128)(2,1)S(1)} reshape(bf16[1,128,2,512]{3,2,1,0:T(2,128)(2,1)} %param.4) | data formatting | bytes 524288 | tf_op jit(solution)/shard_map/reshape;squeeze | solution.py:275
  1.2 0.0 copy-start.1
  1.2 0.0 copy-done
  1.3 0.6 %copy-done.1 = s32[1,64]{1,0:T(1,128)S(1)} copy-done((s32[1,64]{1,0:T(1,128)S(1)}, s32[1,64]{1,0:T(1,128)}, u32[]{:S(2)}) %copy-start.1) | copy-done | bytes 280
  1.9 59.6 %attend.1 = bf16[128,2048]{1,0:T(8,128)(2,1)S(1)} custom-call(s32[1,64]{1,0:T(1,128)S(1)} %copy-done.1, bf16[128,2048]{1,0:T(8,128)(2,1)S(1)} %bitcast.7, bf16[4,2,2,64,128]{4,3,2,1,0:T(8,128)(2,1)S(1)} %bitcast.6), custom_call_target="tpu_custom_call" | custom-call | flops 4294967296 | bytes 4194304 | tf_op jit(solution)/shard_map/attend/pallas_call | solution.py:279
  61.5 0.8 %copy.11 = bf16[1,128,2048]{2,1,0:T(8,128)(2,1)} copy(bf16[1,128,2048]{2,1,0:T(8,128)(2,1)S(1)} %bitcast.5) | data formatting | bytes 1048576
  (1 shorter events, 0.0 us)
Async XLA Ops:
  0.0 1.2 %copy-start = (bf16[1,128,2048]{2,1,0:T(8,128)(2,1)S(1)}, bf16[1,128,2048]{2,1,0:T(8,128)(2,1)}, u32[]{:S(2)}) copy-start(bf16[1,128,2048]{2,1,0:T(8,128)(2,1)} %param.3) | copy-start | bytes 1572868
  1.2 0.7 %copy-start.1 = (s32[1,64]{1,0:T(1,128)S(1)}, s32[1,64]{1,0:T(1,128)}, u32[]{:S(2)}) copy-start(s32[1,64]{1,0:T(1,128)} %ids_ref.1) | copy-start | bytes 772

commit v3 on v2

--- a/solution.py
+++ b/solution.py
@@ -134,7 +134,7 @@
     def product(a, b):
         return lax.dot_general(a, b, (((1,), (1,)), ((), ())), preferred_element_type=jnp.float32)
 
-    def update(yq, rows, scores, values):
+    def soften(yq, rows, scores):
         best = scores[0]
         for s in scores[1:]:
             best = jnp.maximum(best, s)
@@ -142,39 +142,58 @@
         new = jnp.maximum(old, jnp.max(best, axis=-1, keepdims=True))
         shrink = jnp.exp2((old - new) * FACTOR)
         wide = jnp.concatenate([new] * (keys // DIM), axis=-1)
-        weighted = acc[yq, rows] * shrink
         summed = total[yq, rows] * shrink
-        for s, v in zip(scores, values):
+        weights = []
+        for s in scores:
             p = jnp.exp2((s - wide) * FACTOR)
             for k in range(keys // DIM):
                 summed = summed + p[:, k * DIM : (k + 1) * DIM]
-            weighted = weighted + jnp.dot(p.astype(jnp.bfloat16), v, preferred_element_type=jnp.float32)
-        acc[yq, rows] = weighted
+            weights.append(p.astype(jnp.bfloat16))
         total[yq, rows] = summed
         top[yq, rows] = new
-
-    def attend(yq, zz):
+        return weights, shrink
+
+    def attend(yqs, zz):
         low_k, high_k, low_v, high_v = (
             kv_buf[zz, a, b].reshape(keys, DIM) for a in range(2) for b in range(2)
         )
-        low_q, high_q = (
-            jnp.concatenate(
-                [q_buf[yq, b * SPAN : (b + 1) * SPAN, g * DIM : (g + 1) * DIM] for g in range(GROUP)], axis=0
-            )
+        lows, highs = (
+            [
+                q_buf[yq, b * SPAN : (b + 1) * SPAN, g * DIM : (g + 1) * DIM]
+                for yq in yqs
+                for g in range(GROUP)
+            ]
             for b in range(2)
         )
-        home = 2 * (yq * nz + z)
-
-        def masked(s, half):
-            distance = jnp.concatenate([gap[zz, half]] * GROUP, axis=0)
-            return jnp.where(distance <= ids_ref[0, home + half] * SPAN, s, NEG)
-
-        half_rows = GROUP * SPAN
-        update(yq, pl.ds(0, half_rows), [masked(product(low_q, low_k), 0)], [low_v])
-        update(
-            yq, pl.ds(half_rows, half_rows),
-            [product(high_q, low_k), masked(product(high_q, high_k), 1)], [low_v, high_v],
-        )
+        half = GROUP * SPAN
+        rows = len(yqs) * half
+        by_low = product(jnp.concatenate(lows + highs, axis=0), low_k)
+        by_high = product(jnp.concatenate(highs, axis=0), high_k)
+
+        def masked(s, yq, b):
+            distance = jnp.concatenate([gap[zz, b]] * GROUP, axis=0)
+            return jnp.where(distance <= ids_ref[0, 2 * (yq * nz + z) + b] * SPAN, s, NEG)
+
+        p_low, p_high_low, p_high, shrinks = [], [], [], []
+        for n, yq in enumerate(yqs):
+            part = slice(n * half, (n + 1) * half)
+            (p,), shrink_low = soften(yq, pl.ds(0, half), [masked(by_low[part], yq, 0)])
+            scores = [by_low[rows + n * half : rows + (n + 1) * half], masked(by_high[part], yq, 1)]
+            (p1, p2), shrink_high = soften(yq, pl.ds(half, half), scores)
+            p_low.append(p)
+            p_high_low.append(p1)
+            p_high.append(p2)
+            shrinks.append((shrink_low, shrink_high))
+        from_low = jnp.dot(jnp.concatenate(p_low + p_high_low, axis=0), low_v, preferred_element_type=jnp.float32)
+        from_high = jnp.dot(jnp.concatenate(p_high, axis=0), high_v, preferred_element_type=jnp.float32)
+        for n, yq in enumerate(yqs):
+            part = slice(n * half, (n + 1) * half)
+            acc[yq, pl.ds(0, half)] = acc[yq, pl.ds(0, half)] * shrinks[n][0] + from_low[part]
+            acc[yq, pl.ds(half, half)] = (
+                acc[yq, pl.ds(half, half)] * shrinks[n][1]
+                + from_low[rows + n * half : rows + (n + 1) * half]
+                + from_high[part]
+            )
 
     rightward = (3 * nz - 2 - 2 * z) // (2 * nz)
     shorter = rightward * z + (1 - rightward) * (nz - 1 - z)
@@ -209,7 +228,10 @@
             def _():
                 remote(q_buf.at[yy], q_buf.at[yy], q_recv.at[yy], q_recv.at[yy], device(y, z)).wait_recv()
 
-            attend(yy, column(step - 1))
+            @pl.when(j % 2 == 1)
+            def _():
+                attend([other(gray(j - 1)), yy], column(step - 1))
+
             return inner
 
         return lax.fori_loop(0, HEADS, part, carry)
@@ -218,7 +240,11 @@
 
     def finish(j, carry):
         yq = other(gray(HEADS - 1 - j))
-        attend(yq, column(nz - 1))
+
+        @pl.when(j % 2 == 0)
+        def _():
+            attend([yq, other(gray(HEADS - 2 - j))], column(nz - 1))
+
         out = acc[yq] / jnp.sum(total[yq], axis=-1, keepdims=True)
         out = out.astype(jnp.bfloat16)
         for b in range(2):

time: 62.5 us -> 62.5 us (level)
  no operation moved by 1% of the time
where the time goes in v3:
time: 62.5 us; the launch traced here: 62.3 us
  Pallas kernels  59.6 us (95%)
  local copies, waits for them, and re-layouts  2.66 us (4%)
    pallas_call x1, Pallas kernels, per_device(): pl.pallas_call(functools.partial(kernel, nz), out_shape=jax.ShapeDtypeStr...  59.6 us
    unnamed x5, local copies, waits for them, and re-layouts  1.44 us

profile of v3, /device:TPU:8, one launch (start us, length us, event | category | flops | bytes accessed | tf_op | source)
XLA Modules:
  0.0 62.3 jit_solution(13795300899561448493)
XLA Ops:
  0.0 0.0 copy-start
  0.0 1.2 %reshape = bf16[2,64,2,4,128]{4,3,2,1,0:T(4,128)(2,1)S(1)} reshape(bf16[1,128,2,512]{3,2,1,0:T(2,128)(2,1)} %param.4) | data formatting | bytes 524288 | tf_op jit(solution)/shard_map/reshape;squeeze | solution.py:301
  1.2 0.0 copy-start.1
  1.2 0.0 copy-done
  1.3 0.6 %copy-done.1 = s32[1,64]{1,0:T(1,128)S(1)} copy-done((s32[1,64]{1,0:T(1,128)S(1)}, s32[1,64]{1,0:T(1,128)}, u32[]{:S(2)}) %copy-start.1) | copy-done | bytes 280
  1.9 59.6 %attend.1 = bf16[128,2048]{1,0:T(8,128)(2,1)S(1)} custom-call(s32[1,64]{1,0:T(1,128)S(1)} %copy-done.1, bf16[128,2048]{1,0:T(8,128)(2,1)S(1)} %bitcast.7, bf16[4,2,2,64,128]{4,3,2,1,0:T(8,128)(2,1)S(1)} %bitcast.6), custom_call_target="tpu_custom_call" | custom-call | flops 4294967296 | bytes 4194304 | tf_op jit(solution)/shard_map/attend/pallas_call | solution.py:305
  61.5 0.8 %copy.11 = bf16[1,128,2048]{2,1,0:T(8,128)(2,1)} copy(bf16[1,128,2048]{2,1,0:T(8,128)(2,1)S(1)} %bitcast.5) | data formatting | bytes 1048576
  (1 shorter events, 0.0 us)
Async XLA Ops:
  0.0 1.2 %copy-start = (bf16[1,128,2048]{2,1,0:T(8,128)(2,1)S(1)}, bf16[1,128,2048]{2,1,0:T(8,128)(2,1)}, u32[]{:S(2)}) copy-start(bf16[1,128,2048]{2,1,0:T(8,128)(2,1)} %param.3) | copy-start | bytes 1572868
  1.2 0.7 %copy-start.1 = (s32[1,64]{1,0:T(1,128)S(1)}, s32[1,64]{1,0:T(1,128)}, u32[]{:S(2)}) copy-start(s32[1,64]{1,0:T(1,128)} %ids_ref.1) | copy-start | bytes 772

commit v4 on v3

--- a/solution.py
+++ b/solution.py
@@ -23,8 +23,8 @@
 
 
 def kernel(
-    nz, ids_ref, q_ref, kv_ref, out_ref,
-    kv_buf, q_buf, o_buf, gap, acc, total, top,
+    nz, ids_in, q_ref, kv_ref, out_ref,
+    ids_ref, kv_buf, q_buf, o_buf, gap, acc, total, top,
     recv, right_sem, left_sem, kv_sem, q_sem, q_recv, o_sem, o_recv, own_sem,
 ):
     me = lax.axis_index("ctx")
@@ -84,10 +84,12 @@
 
     kv_sends = [
         remote(kv_ref.at[other(d)], piece(z, y), kv_sem.at[d - 1], recv.at[z, y], device(other(d), z))
-        for d in (1, 3, 2)
+        for d in (2, 1, 3)
     ]
     for copy in kv_sends:
         copy.start()
+    ids_copy = pltpu.make_async_copy(ids_in, ids_ref, own_sem.at[3])
+    ids_copy.start()
     own_kv = pltpu.make_async_copy(kv_ref.at[y], piece(z, y), own_sem.at[0])
     own_kv.start()
     q_sends = [
@@ -111,6 +113,8 @@
         @pl.when(has_left)
         def _():
             to_left(piece(z, other(d)), z, other(d)).start()
+
+    ids_copy.wait()
 
     lane = lax.broadcasted_iota(jnp.int32, (SPAN, keys), 1)
     row = lax.broadcasted_iota(jnp.int32, (SPAN, keys), 0)
@@ -306,12 +310,13 @@
         functools.partial(kernel, nz),
         out_shape=jax.ShapeDtypeStruct(q.shape, jnp.bfloat16),
         in_specs=[
-            pl.BlockSpec(memory_space=pltpu.SMEM),
+            pl.BlockSpec(memory_space=pltpu.HBM),
             pl.BlockSpec(memory_space=pl.ANY),
             pl.BlockSpec(memory_space=pl.ANY),
         ],
         out_specs=pl.BlockSpec(memory_space=pl.ANY),
         scratch_shapes=[
+            pltpu.SMEM(span_ids.shape, jnp.int32),
             pltpu.VMEM((nz, 2, 2, HEADS, SPAN, DIM), jnp.bfloat16),
             pltpu.VMEM((HEADS, ROWS, GROUP * DIM), jnp.bfloat16),
             pltpu.VMEM((HEADS, ROWS, GROUP * DIM), jnp.bfloat16),
@@ -320,10 +325,10 @@
             pltpu.VMEM((HEADS, rows, DIM), jnp.float32),
             pltpu.VMEM((HEADS, rows, DIM), jnp.float32),
             dma((nz, HEADS)), dma((nz, HEADS)), dma((nz, HEADS)),
-            dma((3,)), dma((3,)), dma((HEADS,)), dma((HEADS,)), dma((HEADS,)), dma((3,)),
+            dma((3,)), dma((3,)), dma((HEADS,)), dma((HEADS,)), dma((HEADS,)), dma((4,)),
         ],
         compiler_params=pltpu.CompilerParams(
-            collective_id=0, has_side_effects=True, vmem_limit_bytes=48 * 1024 * 1024
+            collective_id=0, has_side_effects=True, vmem_limit_bytes=60 * 1024 * 1024
         ),
         cost_estimate=pl.CostEstimate(flops=flops, bytes_accessed=4 * 1024 * 1024, transcendentals=0),
         name="attend",

time: 62.5 us -> 64.2 us (1.027)
  the two profiles are of different devices: /device:TPU:8 before, /device:TPU:16 now
where the time goes in v4:
time: 64.2 us; the launch traced here: 64 us
  Pallas kernels  60.2 us (94%)
  local copies, waits for them, and re-layouts  3.76 us (6%)
    pallas_call x1, Pallas kernels, per_device(): pl.pallas_call(functools.partial(kernel, nz), out_shape=jax.ShapeDtypeStr...  60.2 us
    unnamed x1, local copies, waits for them, and re-layouts  1.88 us
    another operation x2, local copies, waits for them, and re-layouts, per_device(): kv = keyvals[0].reshape(2, SPAN, 2, HEADS, DIM).transpose(3, 2, 0, 1, 4)  1.88 us

profile of v4, /device:TPU:16, one launch (start us, length us, event | category | flops | bytes accessed | tf_op | source)
XLA Modules:
  0.0 64.0 jit_solution(8169745863371960672)
XLA Ops:
  0.0 1.1 %reshape = bf16[2,64,2,4,128]{4,3,2,1,0:T(4,128)(2,1)S(1)} reshape(bf16[1,128,2,512]{3,2,1,0:T(2,128)(2,1)} %param.4) | data formatting | bytes 524288 | tf_op jit(solution)/shard_map/reshape;squeeze | solution.py:305
  1.1 0.8 %copy.9 = bf16[2,64,2,4,128]{4,1,0,2,3:T(8,128)(2,1)} copy(bf16[2,64,2,4,128]{4,3,2,1,0:T(4,128)(2,1)S(1)} %reshape) | data formatting | bytes 524288 | tf_op jit(solution)/shard_map/reshape;squeeze | solution.py:305
  1.9 60.2 %attend.1 = bf16[128,2048]{1,0:T(8,128)(2,1)} custom-call(s32[1,64]{1,0:T(1,128)} %ids_in.1, bf16[128,2048]{1,0:T(8,128)(2,1)} %bitcast.7, bf16[4,2,2,64,128]{4,3,2,1,0:T(8,128)(2,1)} %bitcast.6), custom_call_target="tpu_custom_call" | custom-call | flops 4294967296 | bytes 4194304 | tf_op jit(solution)/shard_map/attend/pallas_call | solution.py:309
  62.1 1.9 %copy.11 = bf16[1,128,2048]{2,1,0:T(8,128)(2,1)} copy(bf16[1,128,2048]{2,1,0:T(8,128)(2,1)} %bitcast.5) | data formatting | bytes 1048576
